TPU v7x, 32 devices: a whole 2x2x4 slice. The times are simulated.
32 devices in a mesh: gx: 2 (over core), gy: 4 (over y, x), gz: 4 (over z).
Axes of the slice: x: 2, y: 2, z: 4, core: 2. Of those that a mesh axis runs over, the one named last changes fastest.
Arguments:
- features: bfloat16 [4096, 512], P(('gx', 'gy', 'gz')), may hold values from -6 to 6
- halo_index: int32 [3072], P(('gx', 'gy', 'gz')), may hold values from 0 to 127
- edge_src: int32 [128, 384], P(('gx', 'gy', 'gz')), may hold values from 0 to 2623
- edge_dst: int32 [128, 384], P(('gx', 'gy', 'gz')), may hold values from 0 to 127
- edge_count: int32 [128], P(('gx', 'gy', 'gz')), may hold values from 48 to 384, as said below
- edge_basis: bfloat16 [49152, 128], P(('gx', 'gy', 'gz')), may hold values from -6 to 6
- w_edge_in: bfloat16 [4, 1152, 1024], P('gz'), may hold values from -0.1875 to 0.1875
- w_edge_out: bfloat16 [4, 1024, 512], P('gz'), may hold values from -0.1875 to 0.1875
- w_update: bfloat16 [512, 512], replicated, may hold values from -0.25 to 0.25
Outputs:
- new_features: bfloat16 [4096, 512], P(('gx', 'gy', 'gz'))
- halo_next: bfloat16 [832, 96, 512], P(('gx', 'gy', 'gz'))
Inputs may be any that keep to these rules, and one draw needn't show every extreme that they name: The first edge_count slots of a domain's 384 slots for a species pair are live; in every draw some species pair has all 384 slots live in every domain of one gz group.
All inputs are finite; a program needn't handle non-finite values.
Results may differ from a plain program's by a relative error of at most 0.0051.
Values may be sent and summed in bfloat16 or wider, within the bound.
A program may use at most 128 MiB of HBM per device.

v0:
```python
import jax
import jax.numpy as jnp
from jax import lax
from jax.sharding import PartitionSpec as P


def extended(x, sides, width):
    for axis, dim in sides:
        count, length = (lax.axis_size(axis), x.shape[dim])
        up = [(i, (i + 1) % count) for i in range(count)]
        down = [(j, i) for i, j in up]
        last = lax.slice_in_dim(x, length - width, length, axis=dim)
        first = lax.slice_in_dim(x, 0, width, axis=dim)
        before = lax.ppermute(last, axis, up)
        after = lax.ppermute(first, axis, down)
        x = jnp.concatenate([before, x, after], axis=dim)
    return x


def outer_cells(padded):
    flat = padded.reshape(27, padded.shape[3], padded.shape[4])
    return jnp.concatenate([flat[:13], flat[14:]], axis=0)


def shards(
    features,
    halo_index,
    edge_src,
    edge_dst,
    edge_count,
    edge_basis,
    w_edge_in,
    w_edge_out,
    w_update,
):
    model_width = features.shape[1]
    atom_count = features.shape[0]
    group_count = edge_src.shape[0]
    slot_count = edge_src.shape[1]
    first_layer = w_edge_in[0]
    w_source = first_layer[:model_width]
    w_target = first_layer[model_width : 2 * model_width]
    w_radial = first_layer[2 * model_width :]
    w_second = w_edge_out[0]
    boundary = features[halo_index]
    padded = extended(boundary[None, None, None], (("gx", 0), ("gy", 1), ("gz", 2)), 1)
    table_rows = jnp.concatenate([features, outer_cells(padded).reshape(-1, model_width)], axis=0)
    slot_index = lax.broadcasted_iota(jnp.int32, (group_count, slot_count), 1)
    dst_live = jnp.where(slot_index < edge_count[:, None], edge_dst, -1)
    src_rows = table_rows[edge_src]
    basis_rows = edge_basis.reshape(group_count, slot_count, -1)
    owners = lax.all_gather(features, "gz", axis=0, tiled=True)
    source_part = lax.all_to_all(src_rows, "gz", split_axis=0, concat_axis=0, tiled=True)
    radial_part = lax.all_to_all(basis_rows, "gz", split_axis=0, concat_axis=0, tiled=True)
    target_part = lax.all_to_all(dst_live, "gz", split_axis=0, concat_axis=0, tiled=True)
    owner_index = lax.broadcasted_iota(jnp.int32, target_part.shape, 0)
    row_index = owner_index * atom_count + jnp.maximum(target_part, 0)
    pre = jnp.einsum("ock,kh->och", source_part, w_source, preferred_element_type=jnp.float32)
    pre = pre + jnp.einsum(
        "ock,kh->och", owners[row_index], w_target, preferred_element_type=jnp.float32
    )
    pre = pre + jnp.einsum("ock,kh->och", radial_part, w_radial, preferred_element_type=jnp.float32)
    hidden = jax.nn.silu(pre).astype(jnp.bfloat16)
    messages = jnp.einsum(
        "och,hd->ocd", hidden, w_second, preferred_element_type=jnp.float32
    ).astype(jnp.bfloat16)
    atom_iota = lax.broadcasted_iota(jnp.int32, (1, atom_count, 1), 1)
    incidence = (target_part[:, None, :] == atom_iota).astype(jnp.bfloat16)
    partial_value = jnp.einsum(
        "oac,ocd->oad", incidence, messages, preferred_element_type=jnp.float32
    )
    returned = lax.all_to_all(partial_value, "gz", split_axis=0, concat_axis=0, tiled=True)
    summed = jnp.sum(returned, axis=0)
    mean_square = jnp.mean(summed * summed, axis=-1, keepdims=True)
    normed = (summed * lax.rsqrt(mean_square + 1e-05)).astype(jnp.bfloat16)
    update = jnp.dot(normed, w_update, preferred_element_type=jnp.float32)
    new_rows = (features.astype(jnp.float32) + update).astype(jnp.bfloat16)
    boundary_next = new_rows[halo_index]
    padded_next = extended(boundary_next[None, None, None], (("gx", 0), ("gy", 1), ("gz", 2)), 1)
    return (new_rows, outer_cells(padded_next))


def solution(mesh):
    in_specs = (
        P(("gx", "gy", "gz"), None),
        P(("gx", "gy", "gz")),
        P(("gx", "gy", "gz"), None),
        P(("gx", "gy", "gz"), None),
        P(("gx", "gy", "gz")),
        P(("gx", "gy", "gz"), None),
        P("gz", None, None),
        P("gz", None, None),
        P(),
    )
    out_specs = (P(("gx", "gy", "gz"), None), P(("gx", "gy", "gz"), None, None))
    return jax.shard_map(shards, mesh=mesh, in_specs=in_specs, out_specs=out_specs, check_vma=False)
```

profile of v0, /device:TPU:1, one launch (start us, length us, event | category | flops | bytes accessed | tf_op | source)
XLA Modules:
  0.0 242.3 jit_solution(17518737411660622284)
XLA Ops:
  1.4 1.7 gather_fusion
  4.7 3.6 %collective-permute-start.3 = (bf16[3,1,1,96,512]{4,3,2,1,0:T(8,128)(2,1)S(1)}, bf16[3,1,1,96,512]{4,3,2,1,0:T(8,128)(2,1)S(1)}, u32[]{:S(2)}, u32[]{:S(2)}) collective-permute-start(bf16[3,1,1,96,512]{4,3,2,1,0:T(8,128)(2,1)S(1)} %pad_maximum_fusion.7), channel_id=1, source_target_pairs={{4,0},{8,4},{12,8},{0,12},{5,1},{9,5},{13,9},{1,13},{6,2},{10,6},{... | collective-permute-start | bytes 884744 | tf_op jit(solution)/shard_map/ppermute | solution.py:15
  8.3 6.3 %collective-permute-done.3 = bf16[3,1,1,96,512]{4,3,2,1,0:T(8,128)(2,1)S(1)} collective-permute-done((bf16[3,1,1,96,512]{4,3,2,1,0:T(8,128)(2,1)S(1)}, bf16[3,1,1,96,512]{4,3,2,1,0:T(8,128)(2,1)S(1)}, u32[]{:S(2)}, u32[]{:S(2)}) %collective-permute-start.3) | collective-permute-done | bytes 294944 | tf_op jit(solution)/shard_map/ppermute | solution.py:15
  14.5 7.2 %collective-permute-done.2 = bf16[3,1,1,96,512]{4,3,2,1,0:T(8,128)(2,1)S(1)} collective-permute-done((bf16[3,1,1,96,512]{4,3,2,1,0:T(8,128)(2,1)S(1)}, bf16[3,1,1,96,512]{4,3,2,1,0:T(8,128)(2,1)S(1)}, u32[]{:S(2)}, u32[]{:S(2)}) %collective-permute-start.2) | collective-permute-done | bytes 294944 | tf_op jit(solution)/shard_map/ppermute | solution.py:14
  21.9 3.4 %collective-permute-start.5 = (bf16[3,3,1,96,512]{4,3,2,1,0:T(8,128)(2,1)S(1)}, bf16[3,3,1,96,512]{4,3,2,1,0:T(8,128)(2,1)S(1)}, u32[]{:S(2)}, u32[]{:S(2)}) collective-permute-start(bf16[3,3,1,96,512]{4,3,2,1,0:T(8,128)(2,1)S(1)} %pad_maximum_fusion.5), channel_id=1, source_target_pairs={{1,0},{2,1},{3,2},{0,3},{5,4},{6,5},{7,6},{4,7},{9,8},{10,9},{11,1... | collective-permute-start | bytes 2654216 | tf_op jit(solution)/shard_map/ppermute | solution.py:15
  26.0 4.5 %all-to-all-start = ((s32[4,1,384]{2,1,0:T(1,128)}), s32[4,1,384]{2,1,0:T(1,128)S(1)}, u32[]{:S(2)}, u32[]{:S(2)}) async-start(s32[4,1,384]{2,1,0:T(1,128)} %all_to_all.15), calls=%async_computation | async-start | bytes 12288 | tf_op jit(solution)/shard_map/all_to_all | solution.py:55
  30.5 12.8 %collective-permute-done.5 = bf16[3,3,1,96,512]{4,3,2,1,0:T(8,128)(2,1)S(1)} collective-permute-done((bf16[3,3,1,96,512]{4,3,2,1,0:T(8,128)(2,1)S(1)}, bf16[3,3,1,96,512]{4,3,2,1,0:T(8,128)(2,1)S(1)}, u32[]{:S(2)}, u32[]{:S(2)}) %collective-permute-start.5) | collective-permute-done | bytes 884768 | tf_op jit(solution)/shard_map/ppermute | solution.py:15
  43.4 19.9 %collective-permute-done.4 = bf16[3,3,1,96,512]{4,3,2,1,0:T(8,128)(2,1)} collective-permute-done((bf16[3,3,1,96,512]{4,3,2,1,0:T(8,128)(2,1)S(1)}, bf16[3,3,1,96,512]{4,3,2,1,0:T(8,128)(2,1)}, u32[]{:S(2)}, u32[]{:S(2)}) %collective-permute-start.4) | collective-permute-done | bytes 884768 | tf_op jit(solution)/shard_map/ppermute | solution.py:14
  65.8 1.7 pad_maximum_fusion
  67.5 7.6 %gather_fusion.1 = bf16[1536,512]{1,0:T(8,128)(2,1)} fusion(bf16[2624,512]{1,0:T(8,128)(2,1)} %pad_maximum_fusion, s32[2048]{0:T(1024)S(1)} %pad_clamp_fusion.1), kind=kCustom, calls=%fused_computation.1 | custom fusion | bytes 3151872 | tf_op jit(solution)/shard_map/gather | solution.py:50
  75.1 3.6 %all-to-all-start.1 = ((bf16[4,384,512]{2,1,0:T(8,128)(2,1)}), bf16[4,384,512]{2,1,0:T(8,128)(2,1)S(1)}, u32[]{:S(2)}, u32[]{:S(2)}) async-start(bf16[4,384,512]{2,1,0:T(8,128)(2,1)} %bitcast.3), calls=%async_computation.1 | async-start | bytes 3145728 | tf_op jit(solution)/shard_map/all_to_all | solution.py:53
  78.6 44.4 %all_gather.3 = bf16[512,512]{1,0:T(8,128)(2,1)S(1)} all-gather(bf16[128,512]{1,0:T(8,128)(2,1)S(1)} %copy-done.1), channel_id=1, replica_groups=mesh['gx'=2,'gy'=4,'gz'=4] {'gz'}, dimensions={0}, use_global_device_ids=true | all-gather | bytes 655360 | tf_op jit(solution)/shard_map/all_gather | solution.py:52
  123.1 5.4 %gather_fusion.2 = bf16[1536,512]{1,0:T(8,128)(2,1)} fusion(bf16[512,512]{1,0:T(8,128)(2,1)S(1)} %all_gather.3, s32[2048]{0:T(1024)S(1)} %pad_clamp_fusion), kind=kCustom, calls=%fused_computation.2 | custom fusion | bytes 3151872 | tf_op jit(solution)/shard_map/gather | solution.py:60
  128.6 3.7 %all-to-all-start.2 = ((bf16[4,384,128]{2,1,0:T(8,128)(2,1)}), bf16[4,384,128]{2,1,0:T(8,128)(2,1)S(1)}, u32[]{:S(2)}, u32[]{:S(2)}) async-start(bf16[4,384,128]{2,1,0:T(8,128)(2,1)} %bitcast.51), calls=%async_computation.2 | async-start | bytes 786432 | tf_op jit(solution)/shard_map/all_to_all | solution.py:54
  132.3 6.2 %fusion.6 = f32[4,384,1024]{2,1,0:T(8,128)} fusion(bf16[4,384,512]{2,1,0:T(8,128)(2,1)} %bitcast.40, bf16[1,1152,1024]{2,1,0:T(8,128)(2,1)} %param.15), kind=kOutput, calls=%fused_computation.16 | convolution fusion | flops 1610612736 | bytes 8912896 | tf_op jit(solution)/shard_map/ock,kh->och/dot_general | solution.py:59
  138.5 5.6 %fusion.8 = f32[4,384,1024]{2,1,0:T(8,128)} fusion(bf16[4,384,512]{2,1,0:T(8,128)(2,1)S(1)} %all-to-all-done.1, bf16[1,1152,1024]{2,1,0:T(8,128)(2,1)} %param.15), kind=kOutput, calls=%fused_computation.18 | convolution fusion | flops 1610612736 | bytes 8912896 | tf_op jit(solution)/shard_map/ock,kh->och/dot_general | solution.py:58
  144.1 8.0 %fusion.3 = bf16[4,384,512]{2,1,0:T(8,128)(2,1)S(1)} fusion(f32[4,384,1024]{2,1,0:T(8,128)} %fusion.8, f32[4,384,1024]{2,1,0:T(8,128)} %fusion.6, bf16[4,384,128]{2,1,0:T(8,128)(2,1)S(1)} %all-to-all-done.2, bf16[1,1024,512]{2,1,0:T(8,128)(2,1)S(1)} %copy-done, bf16[1,1152,1024]{2,1,0:T(8,128)(2,1)} %param.15), kind=kOutput, calls=%fused_computation.12 | convolution fusion | flops 2025062400 | bytes 15859712 | tf_op jit(solution)/shard_map/och,hd->ocd/dot_general | solution.py:64
  152.5 27.7 %all_to_all.24 = f32[4,128,512]{2,1,0:T(8,128)S(1)} all-to-all(f32[4,128,512]{2,1,0:T(8,128)S(1)} %fusion.12), channel_id=1, replica_groups=mesh['gx'=2,'gy'=4,'gz'=4] {'gz'}, dimensions={0} | all-to-all | bytes 2097152 | tf_op jit(solution)/shard_map/all_to_all | solution.py:72
  181.6 3.4 %collective-permute-start.7 = (bf16[1,1,1,96,512]{4,3,2,1,0:T(8,128)(2,1)S(1)}, bf16[1,1,1,96,512]{4,3,2,1,0:T(8,128)(2,1)S(1)}, u32[]{:S(2)}, u32[]{:S(2)}) collective-permute-start(bf16[1,1,1,96,512]{4,3,2,1,0:T(8,128)(2,1)S(1)} %bitcast.46), channel_id=1, source_target_pairs={{16,0},{0,16},{17,1},{1,17},{18,2},{2,18},{19,3},{3,19},{20,4},{4,... | collective-permute-start | bytes 294920 | tf_op jit(solution)/shard_map/ppermute | solution.py:15
  187.8 6.9 %collective-permute-done.9 = bf16[3,1,1,96,512]{4,3,2,1,0:T(8,128)(2,1)S(1)} collective-permute-done((bf16[3,1,1,96,512]{4,3,2,1,0:T(8,128)(2,1)S(1)}, bf16[3,1,1,96,512]{4,3,2,1,0:T(8,128)(2,1)S(1)}, u32[]{:S(2)}, u32[]{:S(2)}) %collective-permute-start.9) | collective-permute-done | bytes 294944 | tf_op jit(solution)/shard_map/ppermute | solution.py:15
  194.7 6.3 %collective-permute-done.8 = bf16[3,1,1,96,512]{4,3,2,1,0:T(8,128)(2,1)S(1)} collective-permute-done((bf16[3,1,1,96,512]{4,3,2,1,0:T(8,128)(2,1)S(1)}, bf16[3,1,1,96,512]{4,3,2,1,0:T(8,128)(2,1)S(1)}, u32[]{:S(2)}, u32[]{:S(2)}) %collective-permute-start.8) | collective-permute-done | bytes 294944 | tf_op jit(solution)/shard_map/ppermute | solution.py:14
  202.6 18.9 %collective-permute-done.11 = bf16[3,3,1,96,512]{4,3,2,1,0:T(8,128)(2,1)S(1)} collective-permute-done((bf16[3,3,1,96,512]{4,3,2,1,0:T(8,128)(2,1)S(1)}, bf16[3,3,1,96,512]{4,3,2,1,0:T(8,128)(2,1)S(1)}, u32[]{:S(2)}, u32[]{:S(2)}) %collective-permute-start.11) | collective-permute-done | bytes 884768 | tf_op jit(solution)/shard_map/ppermute | solution.py:15
  221.5 18.6 %collective-permute-done.10 = bf16[3,3,1,96,512]{4,3,2,1,0:T(8,128)(2,1)S(1)} collective-permute-done((bf16[3,3,1,96,512]{4,3,2,1,0:T(8,128)(2,1)S(1)}, bf16[3,3,1,96,512]{4,3,2,1,0:T(8,128)(2,1)S(1)}, u32[]{:S(2)}, u32[]{:S(2)}) %collective-permute-start.10) | collective-permute-done | bytes 884768 | tf_op jit(solution)/shard_map/ppermute | solution.py:14
  240.6 1.7 pad_maximum_fusion.4
  (61 shorter events, 12.4 us)
Async XLA Ops:
  0.6 143.5 %copy-start = (bf16[1,1024,512]{2,1,0:T(8,128)(2,1)S(1)}, bf16[1,1024,512]{2,1,0:T(8,128)(2,1)}, u32[]{:S(2)}) copy-start(bf16[1,1024,512]{2,1,0:T(8,128)(2,1)} %param.16) | copy-start | bytes 3145732
  0.6 24.6 %copy-start.8 = (s32[4]{0:T(128)S(1)}, s32[4]{0:T(128)}, u32[]{:S(2)}) copy-start(s32[4]{0:T(128)} %param.13) | copy-start | bytes 52
  0.7 24.6 %copy-start.6 = (s32[4,384]{1,0:T(4,128)S(1)}, s32[4,384]{1,0:T(4,128)}, u32[]{:S(2)}) copy-start(s32[4,384]{1,0:T(4,128)} %param.12) | copy-start | bytes 18436
  0.7 29.8 %copy-start.7 = (s32[4,384]{1,0:T(4,128)S(1)}, s32[4,384]{1,0:T(4,128)}, u32[]{:S(2)}) copy-start(s32[4,384]{1,0:T(4,128)} %param.11) | copy-start | bytes 18436
  3.1 1.4 collective-permute-start.1
  3.2 1.4 collective-permute-start
  4.5 20.8 %copy-start.3 = (bf16[1,1,1,96,512]{4,3,2,1,0:T(8,128)(2,1)}, bf16[1,1,1,96,512]{4,3,2,1,0:T(8,128)(2,1)S(1)}, u32[]{:S(2)}) copy-start(bf16[1,1,1,96,512]{4,3,2,1,0:T(8,128)(2,1)S(1)} %collective-permute-done.1) | copy-start | bytes 294916
  4.7 20.7 %copy-start.4 = (bf16[1,1,1,96,512]{4,3,2,1,0:T(8,128)(2,1)}, bf16[1,1,1,96,512]{4,3,2,1,0:T(8,128)(2,1)S(1)}, u32[]{:S(2)}) copy-start(bf16[1,1,1,96,512]{4,3,2,1,0:T(8,128)(2,1)S(1)} %collective-permute-done) | copy-start | bytes 294916
  4.7 9.8 %collective-permute-start.3 = (bf16[3,1,1,96,512]{4,3,2,1,0:T(8,128)(2,1)S(1)}, bf16[3,1,1,96,512]{4,3,2,1,0:T(8,128)(2,1)S(1)}, u32[]{:S(2)}, u32[]{:S(2)}) collective-permute-start(bf16[3,1,1,96,512]{4,3,2,1,0:T(8,128)(2,1)S(1)} %pad_maximum_fusion.7), channel_id=1, source_target_pairs={{4,0},{8,4},{12,8},{0,12},{5,1},{9,5},{13,9},{1,13},{6,2},{10,6},{... | collective-permute-start | bytes 884744 | tf_op jit(solution)/shard_map/ppermute | solution.py:15
  8.3 13.5 %collective-permute-start.2 = (bf16[3,1,1,96,512]{4,3,2,1,0:T(8,128)(2,1)S(1)}, bf16[3,1,1,96,512]{4,3,2,1,0:T(8,128)(2,1)S(1)}, u32[]{:S(2)}, u32[]{:S(2)}) collective-permute-start(bf16[3,1,1,96,512]{4,3,2,1,0:T(8,128)(2,1)S(1)} %pad_maximum_fusion.7), channel_id=1, source_target_pairs={{0,4},{4,8},{8,12},{12,0},{1,5},{5,9},{9,13},{13,1},{2,6},{6,10},{... | collective-permute-start | bytes 884744 | tf_op jit(solution)/shard_map/ppermute | solution.py:14
  21.9 21.5 %collective-permute-start.5 = (bf16[3,3,1,96,512]{4,3,2,1,0:T(8,128)(2,1)S(1)}, bf16[3,3,1,96,512]{4,3,2,1,0:T(8,128)(2,1)S(1)}, u32[]{:S(2)}, u32[]{:S(2)}) collective-permute-start(bf16[3,3,1,96,512]{4,3,2,1,0:T(8,128)(2,1)S(1)} %pad_maximum_fusion.5), channel_id=1, source_target_pairs={{1,0},{2,1},{3,2},{0,3},{5,4},{6,5},{7,6},{4,7},{9,8},{10,9},{11,1... | collective-permute-start | bytes 2654216 | tf_op jit(solution)/shard_map/ppermute | solution.py:15
  25.3 38.0 %collective-permute-start.4 = (bf16[3,3,1,96,512]{4,3,2,1,0:T(8,128)(2,1)S(1)}, bf16[3,3,1,96,512]{4,3,2,1,0:T(8,128)(2,1)}, u32[]{:S(2)}, u32[]{:S(2)}) collective-permute-start(bf16[3,3,1,96,512]{4,3,2,1,0:T(8,128)(2,1)S(1)} %pad_maximum_fusion.5), channel_id=1, source_target_pairs={{0,1},{1,2},{2,3},{3,0},{4,5},{5,6},{6,7},{7,4},{8,9},{9,10},{10,1... | collective-permute-start | bytes 2654216 | tf_op jit(solution)/shard_map/ppermute | solution.py:14
  26.0 49.1 %all-to-all-start = ((s32[4,1,384]{2,1,0:T(1,128)}), s32[4,1,384]{2,1,0:T(1,128)S(1)}, u32[]{:S(2)}, u32[]{:S(2)}) async-start(s32[4,1,384]{2,1,0:T(1,128)} %all_to_all.15), calls=%async_computation | async-start | bytes 12288 | tf_op jit(solution)/shard_map/all_to_all | solution.py:55
  64.9 0.9 copy-start.1
  75.1 53.5 %all-to-all-start.1 = ((bf16[4,384,512]{2,1,0:T(8,128)(2,1)}), bf16[4,384,512]{2,1,0:T(8,128)(2,1)S(1)}, u32[]{:S(2)}, u32[]{:S(2)}) async-start(bf16[4,384,512]{2,1,0:T(8,128)(2,1)} %bitcast.3), calls=%async_computation.1 | async-start | bytes 3145728 | tf_op jit(solution)/shard_map/all_to_all | solution.py:53
  128.6 15.5 %all-to-all-start.2 = ((bf16[4,384,128]{2,1,0:T(8,128)(2,1)}), bf16[4,384,128]{2,1,0:T(8,128)(2,1)S(1)}, u32[]{:S(2)}, u32[]{:S(2)}) async-start(bf16[4,384,128]{2,1,0:T(8,128)(2,1)} %bitcast.51), calls=%async_computation.2 | async-start | bytes 786432 | tf_op jit(solution)/shard_map/all_to_all | solution.py:54
  152.1 28.4 %copy-start.5 = (bf16[512,512]{1,0:T(8,128)(2,1)S(1)}, bf16[512,512]{1,0:T(8,128)(2,1)}, u32[]{:S(2)}) copy-start(bf16[512,512]{1,0:T(8,128)(2,1)} %param.17) | copy-start | bytes 1572868
  180.8 59.7 %copy-start.2 = (bf16[128,512]{1,0:T(8,128)(2,1)}, bf16[128,512]{1,0:T(8,128)(2,1)S(1)}, u32[]{:S(2)}) copy-start(bf16[128,512]{1,0:T(8,128)(2,1)S(1)} %fusion.4) | copy-start | bytes 393220
  181.6 4.3 %collective-permute-start.7 = (bf16[1,1,1,96,512]{4,3,2,1,0:T(8,128)(2,1)S(1)}, bf16[1,1,1,96,512]{4,3,2,1,0:T(8,128)(2,1)S(1)}, u32[]{:S(2)}, u32[]{:S(2)}) collective-permute-start(bf16[1,1,1,96,512]{4,3,2,1,0:T(8,128)(2,1)S(1)} %bitcast.46), channel_id=1, source_target_pairs={{16,0},{0,16},{17,1},{1,17},{18,2},{2,18},{19,3},{3,19},{20,4},{4,... | collective-permute-start | bytes 294920 | tf_op jit(solution)/shard_map/ppermute | solution.py:15
  184.9 1.3 collective-permute-start.6
  186.3 8.5 %collective-permute-start.9 = (bf16[3,1,1,96,512]{4,3,2,1,0:T(8,128)(2,1)S(1)}, bf16[3,1,1,96,512]{4,3,2,1,0:T(8,128)(2,1)S(1)}, u32[]{:S(2)}, u32[]{:S(2)}) collective-permute-start(bf16[3,1,1,96,512]{4,3,2,1,0:T(8,128)(2,1)S(1)} %pad_maximum_fusion.8), channel_id=1, source_target_pairs={{4,0},{8,4},{12,8},{0,12},{5,1},{9,5},{13,9},{1,13},{6,2},{10,6},{... | collective-permute-start | bytes 884744 | tf_op jit(solution)/shard_map/ppermute | solution.py:15
  187.5 13.5 %collective-permute-start.8 = (bf16[3,1,1,96,512]{4,3,2,1,0:T(8,128)(2,1)S(1)}, bf16[3,1,1,96,512]{4,3,2,1,0:T(8,128)(2,1)S(1)}, u32[]{:S(2)}, u32[]{:S(2)}) collective-permute-start(bf16[3,1,1,96,512]{4,3,2,1,0:T(8,128)(2,1)S(1)} %pad_maximum_fusion.8), channel_id=1, source_target_pairs={{0,4},{4,8},{8,12},{12,0},{1,5},{5,9},{9,13},{13,1},{2,6},{6,10},{... | collective-permute-start | bytes 884744 | tf_op jit(solution)/shard_map/ppermute | solution.py:14
  201.1 20.4 %collective-permute-start.11 = (bf16[3,3,1,96,512]{4,3,2,1,0:T(8,128)(2,1)S(1)}, bf16[3,3,1,96,512]{4,3,2,1,0:T(8,128)(2,1)S(1)}, u32[]{:S(2)}, u32[]{:S(2)}) collective-permute-start(bf16[3,3,1,96,512]{4,3,2,1,0:T(8,128)(2,1)S(1)} %pad_maximum_fusion.6), channel_id=1, source_target_pairs={{1,0},{2,1},{3,2},{0,3},{5,4},{6,5},{7,6},{4,7},{9,8},{10,9},{11,1... | collective-permute-start | bytes 2654216 | tf_op jit(solution)/shard_map/ppermute | solution.py:15
  202.3 37.8 %collective-permute-start.10 = (bf16[3,3,1,96,512]{4,3,2,1,0:T(8,128)(2,1)S(1)}, bf16[3,3,1,96,512]{4,3,2,1,0:T(8,128)(2,1)S(1)}, u32[]{:S(2)}, u32[]{:S(2)}) collective-permute-start(bf16[3,3,1,96,512]{4,3,2,1,0:T(8,128)(2,1)S(1)} %pad_maximum_fusion.6), channel_id=1, source_target_pairs={{0,1},{1,2},{2,3},{3,0},{4,5},{5,6},{6,7},{7,4},{8,9},{9,10},{10,1... | collective-permute-start | bytes 2654216 | tf_op jit(solution)/shard_map/ppermute | solution.py:14
where the time goes:
time: 245 us; the launch traced here: 242 us
  waiting for transfers between devices  99.1 us (40%)
  blocking collectives  72.1 us (29%)
  starting transfers between devices  25.8 us (11%)
  matrix products  20.5 us (8%)
  local copies, waits for them, and re-layouts  17.2 us (7%)
  other arithmetic  6.8 us (3%)
    ppermute x6, waiting for transfers between devices, extended(): before = lax.ppermute(last, axis, up)  52.5 us
    ppermute x6, waiting for transfers between devices, extended(): after = lax.ppermute(first, axis, down)  46.6 us
    all_gather x1, blocking collectives, shards(): owners = lax.all_gather(features, 'gz', axis=0, tiled=True)  44.4 us
    all_to_all x1, blocking collectives, shards(): lax.all_to_all(partial_value, 'gz', split_axis=0, concat_axis=0, tiled=True)  27.7 us
    ppermute x6, starting transfers between devices, extended(): after = lax.ppermute(first, axis, down)  12.8 us
    dot_general x1, matrix products, shards(): jnp.einsum('och,hd->ocd', hidden, w_second, preferred_element_type=jnp.fl...  7.98 us
    gather x1, local copies, waits for them, and re-layouts, shards(): src_rows = table_rows[edge_src]  7.59 us
    dot_general x1, matrix products, shards(): jnp.einsum('ock,kh->och', owners[row_index], w_target, preferred_element_...  6.17 us
  transfers between devices with their start and end apart: 15, of which 12 were waited for; matrix products, arithmetic and copies ran while one was open for 12% of the time, Pallas kernels for 0%

commit v1 on v0

v1 whole, which is shorter than its diff:
```python
import functools

import jax
import jax.numpy as jnp
from jax import lax
from jax.experimental import pallas as pl
from jax.experimental.pallas import tpu as pltpu
from jax.sharding import PartitionSpec as P

AXES = ("gx", "gy", "gz")
MESH = pl.DeviceIdType.MESH


class Place:
    def __init__(self, sizes):
        self.nx, self.ny, self.nz = sizes
        self.x, self.y, self.z = (lax.axis_index(name) for name in AXES)
        x, y, z = self.x, self.y, self.z
        self.first = (x, y + 1 - 2 * lax.rem(y, 2), z)
        self.second = (x, lax.rem(y + 2, 4), z)
        self.b_first = 2 - 2 * lax.rem(y, 2)
        self.b_second = 2 * lax.rem(y, 2)
        self.siblings = [(lax.rem(x + 1, self.nx), y, z)]
        if self.nx > 2:
            self.siblings.append((lax.rem(x + self.nx - 1, self.nx), y, z))

    def along_z(self, step):
        return (self.x, self.y, lax.rem(self.z + step + self.nz, self.nz))

    def sibling_slot(self, index):
        return 1 if self.nx == 2 else 2 - index

    def meet(self):
        barrier = pltpu.get_barrier_semaphore()
        partners = [self.along_z(step) for step in range(1, self.nz)]
        partners += [self.first, self.second] + self.siblings
        for partner in partners:
            pl.semaphore_signal(barrier, inc=1, device_id=partner, device_id_type=MESH)
        pl.semaphore_wait(barrier, len(partners))


def remote(source, target, send, receive, device):
    return pltpu.make_async_remote_copy(
        src_ref=source,
        dst_ref=target,
        send_sem=send,
        recv_sem=receive,
        device_id=device,
        device_id_type=MESH,
    )


def gather_kernel(sizes, f_ref, h_ref, basis_ref, meta_ref, g_ref, hg_ref, bg_ref, mg_ref,
                  send, receive, e_send, e_receive, local):
    place = Place(sizes)
    z, nz = place.z, place.nz
    pairs = ((f_ref, g_ref), (h_ref, hg_ref))
    edge_pairs = ((meta_ref, mg_ref), (basis_ref, bg_ref))

    locals_ = []
    for q, (own, grid) in enumerate(pairs):
        locals_.append(pltpu.make_async_copy(own, grid.at[0, 1, z], local.at[q]))
    for q, (own, grid) in enumerate(edge_pairs):
        locals_.append(pltpu.make_async_copy(own.at[z], grid.at[z], local.at[2 + q]))
    for copy in locals_:
        copy.start()
    place.meet()

    entries = [(0, 0)] + [(s, sign) for s in range(1, nz) for sign in (-1, 1)]

    def when(entry, action):
        s, sign = entry
        zz = z + sign * s
        if s == 0:
            action(zz)
        else:
            pl.when((zz >= 0) & (zz < nz))(functools.partial(action, zz))

    def transfers(s, b, zz, kind, slot, device):
        out = []
        for q, (own, grid) in enumerate(pairs):
            source = own if (s == 0 and kind != 2 and b is None) else grid.at[0, 1 if b is None else b, zz]
            index = 1 if b is None else b
            out.append(remote(source, grid.at[slot[0], slot[1], zz], send.at[q, kind, index, zz],
                              receive.at[q, slot[0], slot[1], zz], device))
        return out

    def to_siblings(s, b, zz):
        out = []
        for i, device in enumerate(place.siblings):
            slot = (place.sibling_slot(i), 1 if b is None else b)
            out += transfers(s, b, zz, 4 + i, slot, device)
        return out

    def arrival(a, b, zz):
        for q, (own, grid) in enumerate(pairs):
            remote(grid.at[a, b, zz], grid.at[a, b, zz], send.at[q, 0, 0, 0],
                   receive.at[q, a, b, zz], place.first).wait_recv()

    def chain(entry, zz, do):
        s, sign = entry
        if s < nz - 1:
            for go in ((1, -1) if s == 0 else (-sign,)):
                device = (place.x, place.y, z + go)

                def act():
                    for copy in transfers(s, None, zz, 0 if go > 0 else 1, (0, 1), device):
                        do(copy)

                pl.when((z + go >= 0) & (z + go < nz))(act)

    def own_stage(entry, do):
        def act(zz):
            if entry[0] > 0 and do is start:
                arrival(0, 1, zz)
            chain(entry, zz, do)
            for copy in transfers(entry[0], None, zz, 2 if entry[0] > 0 else 3, (0, 2 - place.b_first), place.first):
                do(copy)
            for copy in to_siblings(entry[0], None, zz):
                do(copy)

        when(entry, act)

    def first_stage(entry, do):
        def act(zz):
            if do is start:
                arrival(0, place.b_first, zz)
            for copy in transfers(1, place.b_first, zz, 3, (0, place.b_first_of_second), place.second):
                do(copy)
            for copy in to_siblings(1, place.b_first, zz):
                do(copy)

        when(entry, act)

    def second_stage(entry, do):
        def act(zz):
            if do is start:
                arrival(0, place.b_second, zz)
            for copy in to_siblings(1, place.b_second, zz):
                do(copy)

        when(entry, act)

    def edges(do):
        for step in range(1, nz):
            device = place.along_z(step)
            for q, (own, grid) in enumerate(edge_pairs):
                do(remote(own.at[device[2]], grid.at[z], e_send.at[q, step],
                          e_receive.at[q, step], device))

    def start(copy):
        copy.start()

    def finish(copy):
        copy.wait_send()

    place.b_first_of_second = place.b_second
    rounds = [[(0, 0)]] + [[(s, -1), (s, 1)] for s in range(1, nz)]
    for r in range(nz + 2):
        if r < nz:
            for entry in rounds[r]:
                own_stage(entry, start)
        if r == 0:
            edges(start)
        if 1 <= r <= nz:
            for entry in rounds[r - 1]:
                first_stage(entry, start)
        if r >= 2:
            for entry in rounds[r - 2]:
                second_stage(entry, start)

    for copy in locals_:
        copy.wait()
    for entry in entries:
        own_stage(entry, finish)
        first_stage(entry, finish)
        second_stage(entry, finish)
    edges(lambda copy: copy.wait())
    for a in range(1, 1 + len(place.siblings)):
        for b in range(3):
            for zz in range(nz):
                arrival(a, b, zz)


def edge_kernel(nz, halo, g_ref, hg_ref, bg_ref, mg_ref, w1_ref, w2_ref, out_ref, table, w_mix):
    na = g_ref.shape[0]
    atoms, width = g_ref.shape[3:]
    slots = mg_ref.shape[2]
    radial = bg_ref.shape[2]
    lanes = hg_ref.shape[4]
    group = na * 3 * halo
    w_mix[:radial, :] = w1_ref[2 * width :, :]
    rest = table.shape[0] - (nz + 2) * group
    table[(nz + 2) * group :, :] = jnp.zeros((rest, width), jnp.bfloat16)
    lane = lax.broadcasted_iota(jnp.int32, (lanes, lanes), 1).astype(jnp.float32)

    def fill(z, carry):
        for a in range(na):
            for b in range(3):
                index = jnp.broadcast_to(hg_ref[a, b, z, 0:1, :], (lanes, lanes)).T
                pick = (index == lane).astype(jnp.bfloat16)[:halo, :atoms]
                rows = jnp.dot(pick, g_ref[a, b, z], preferred_element_type=jnp.float32).astype(jnp.bfloat16)
                at = (a * 3 + b) * halo
                table[pl.ds(pl.multiple_of((z + 1) * group + at, 16), halo), :] = rows

                @pl.when(z == 0)
                def _():
                    table[pl.ds((nz + 1) * group + at, halo), :] = rows

                @pl.when(z == nz - 1)
                def _():
                    table[pl.ds(at, halo), :] = rows
        return carry

    lax.fori_loop(0, nz, fill, 0)
    window = -(-3 * group // lanes) * lanes
    lane_s = lax.broadcasted_iota(jnp.int32, (slots, lanes), 1).astype(jnp.float32)
    sublane = lax.broadcasted_iota(jnp.int32, (atoms, slots), 0).astype(jnp.float32)

    def domain(o, carry):
        position = jnp.broadcast_to(mg_ref[o, 0:1, :], (lanes, slots)).T
        target = jnp.broadcast_to(mg_ref[o, 1:2, :], (lanes, slots)).T
        own = g_ref[0, 1, o]
        pick = (position == lane_s).astype(jnp.bfloat16)
        source = jnp.dot(pick, own, preferred_element_type=jnp.float32)
        picks = jnp.concatenate(
            [(position - float(atoms + j * lanes) == lane_s).astype(jnp.bfloat16) for j in range(window // lanes)],
            axis=1,
        )
        rows = table[pl.ds(pl.multiple_of(o * group, 16), window), :]
        source = source + jnp.dot(picks, rows, preferred_element_type=jnp.float32)
        w_mix[radial:, :] = jnp.dot(
            own, w1_ref[width : 2 * width, :], preferred_element_type=jnp.float32
        ).astype(jnp.bfloat16)
        mix = jnp.concatenate([bg_ref[o], (target == lane_s).astype(jnp.bfloat16)], axis=1)
        pre = jnp.dot(source.astype(jnp.bfloat16), w1_ref[:width, :], preferred_element_type=jnp.float32)
        pre = pre + jnp.dot(mix, w_mix[...], preferred_element_type=jnp.float32)
        half = 0.5 * pre
        hidden = (half + half * jnp.tanh(half)).astype(jnp.bfloat16)
        incidence = (jnp.broadcast_to(mg_ref[o, 1:2, :], (atoms, slots)) == sublane).astype(jnp.bfloat16)
        summed = jnp.dot(incidence, hidden, preferred_element_type=jnp.float32).astype(jnp.bfloat16)
        out_ref[o] = jnp.dot(summed, w2_ref[...], preferred_element_type=jnp.float32).astype(jnp.bfloat16)
        return carry

    lax.fori_loop(0, nz, domain, 0)


def update_kernel(sizes, halo, part_ref, f_ref, h_ref, w_ref, new_ref, n_ref,
                  landed, edge_rows, p_send, p_receive, send, receive, local):
    place = Place(sizes)
    z, nz = place.z, place.nz
    place.meet()
    copies = []
    for step in range(1, nz):
        device = place.along_z(step)
        copies.append(remote(part_ref.at[device[2]], landed.at[step - 1], p_send.at[step],
                             p_receive.at[step], device))
    for copy in copies:
        copy.start()
    total = part_ref[z].astype(jnp.float32)
    for step, copy in enumerate(copies):
        copy.wait_recv()
        total = total + landed[step].astype(jnp.float32)
    mean_square = jnp.mean(total * total, axis=-1, keepdims=True)
    normed = (total * lax.rsqrt(mean_square + 1e-05)).astype(jnp.bfloat16)
    update = jnp.dot(normed, w_ref[...], preferred_element_type=jnp.float32)
    new_rows = (f_ref[...].astype(jnp.float32) + update).astype(jnp.bfloat16)
    lanes = h_ref.shape[1]
    atoms = f_ref.shape[0]
    lane = lax.broadcasted_iota(jnp.int32, (lanes, lanes), 1).astype(jnp.float32)
    index = jnp.broadcast_to(h_ref[0:1, :], (lanes, lanes)).T
    pick = (index == lane).astype(jnp.bfloat16)[:halo, :atoms]
    edge_rows[...] = jnp.dot(pick, new_rows, preferred_element_type=jnp.float32).astype(jnp.bfloat16)
    new_ref[...] = new_rows

    started = []

    def begin(b, c, kind, slot, device):
        source = edge_rows if (b is None and c == 1) else n_ref.at[0, 1 if b is None else b, c]
        index = 1 if b is None else b
        copy = remote(source, n_ref.at[slot], send.at[kind, index, c], receive.at[slot], device)
        copy.start()
        started.append(copy)

    def arrival(a, b, c):
        remote(n_ref.at[a, b, c], n_ref.at[a, b, c], send.at[0, 0, 0], receive.at[a, b, c], place.first).wait_recv()

    def to_siblings(b, c):
        for i, device in enumerate(place.siblings):
            begin(b, c, 3 + i, (place.sibling_slot(i), 1 if b is None else b, c), device)

    begin(None, 1, 0, (0, 1, 0), place.along_z(1))
    begin(None, 1, 1, (0, 1, 2), place.along_z(-1))
    begin(None, 1, 2, (0, 2 - place.b_first, 1), place.first)
    to_siblings(None, 1)
    own = pltpu.make_async_copy(edge_rows, n_ref.at[0, 1, 1], local)
    own.start()
    order = (1, 0, 2)
    for c in order[1:]:
        arrival(0, 1, c)
        begin(None, c, 2, (0, 2 - place.b_first, c), place.first)
        to_siblings(None, c)
    for c in order:
        arrival(0, place.b_first, c)
        begin(place.b_first, c, 2, (0, place.b_second, c), place.second)
        to_siblings(place.b_first, c)
    for c in order:
        arrival(0, place.b_second, c)
        to_siblings(place.b_second, c)
    for a in range(1, 1 + len(place.siblings)):
        for b in range(3):
            for c in range(3):
                arrival(a, b, c)
    own.wait()
    for copy in copies + started:
        copy.wait_send()


def slots_of(nx):
    return (1, 0, 1) if nx == 2 else (2, 0, 1)


def shards(sizes, features, halo_index, edge_src, edge_dst, edge_count, edge_basis, w_edge_in, w_edge_out, w_update):
    nx, ny, nz = sizes
    atoms, width = features.shape
    groups, slots = edge_src.shape
    halo = halo_index.shape[0]
    radial = edge_basis.shape[1]
    hidden = w_edge_in.shape[2]
    lanes = -(-max(atoms, halo) // 128) * 128
    na = 2 if nx == 2 else 3
    f32, bf16 = jnp.float32, jnp.bfloat16

    index = jnp.pad(halo_index.astype(f32)[None, :], ((0, 7), (0, lanes - halo)), constant_values=-1.0)
    beyond = edge_src - atoms
    offset = beyond // halo
    offset = offset + (offset >= 13)
    off_x, off_y, off_z = offset // 9, (offset // 3) % 3, offset % 3
    slot_x = jnp.where(off_x == 1, 0, jnp.where(off_x == 2, 1, na - 1))
    position = atoms + ((off_z * na + slot_x) * 3 + off_y) * halo + beyond % halo
    position = jnp.where(edge_src < atoms, edge_src, position)
    live = lax.broadcasted_iota(jnp.int32, (groups, slots), 1) < edge_count[:, None]
    target = jnp.where(live, edge_dst, -1)
    meta = jnp.stack([position, target], axis=1).astype(f32)
    meta = jnp.pad(meta, ((0, 0), (0, 6), (0, 0)))
    basis = edge_basis.reshape(groups, slots, radial)

    vmem = pl.BlockSpec(memory_space=pltpu.VMEM)
    anywhere = pl.BlockSpec(memory_space=pl.ANY)
    dma = pltpu.SemaphoreType.DMA
    kinds = 4 + (na - 1)
    grid, index_grid, basis_all, meta_all = pl.pallas_call(
        functools.partial(gather_kernel, sizes),
        out_shape=(
            jax.ShapeDtypeStruct((na, 3, nz, atoms, width), bf16),
            jax.ShapeDtypeStruct((na, 3, nz, 8, lanes), f32),
            jax.ShapeDtypeStruct((nz, slots, radial), bf16),
            jax.ShapeDtypeStruct((nz, 8, slots), f32),
        ),
        in_specs=[anywhere] * 4,
        out_specs=(anywhere,) * 4,
        scratch_shapes=[
            dma((2, kinds, 3, nz)),
            dma((2, na, 3, nz)),
            dma((2, nz)),
            dma((2, nz)),
            dma((4,)),
        ],
        compiler_params=pltpu.CompilerParams(collective_id=0, has_side_effects=True),
        name="gather_blocks",
    )(features, index, basis, meta)

    group = na * 3 * halo
    window = -(-3 * group // lanes) * lanes
    table_rows = (nz - 1) * group + window
    partial_sums = pl.pallas_call(
        functools.partial(edge_kernel, nz, halo),
        out_shape=jax.ShapeDtypeStruct((nz, atoms, width), bf16),
        in_specs=[vmem] * 6,
        out_specs=vmem,
        scratch_shapes=[
            pltpu.VMEM((table_rows, width), bf16),
            pltpu.VMEM((radial + lanes, hidden), bf16),
        ],
        compiler_params=pltpu.CompilerParams(vmem_limit_bytes=60 * 1024 * 1024),
        name="edge_network",
    )(grid, index_grid, basis_all, meta_all, w_edge_in[0], w_edge_out[0])

    new_rows, blocks = pl.pallas_call(
        functools.partial(update_kernel, sizes, halo),
        out_shape=(
            jax.ShapeDtypeStruct((atoms, width), bf16),
            jax.ShapeDtypeStruct((na, 3, 3, halo, width), bf16),
        ),
        in_specs=[vmem] * 4,
        out_specs=(vmem, anywhere),
        scratch_shapes=[
            pltpu.VMEM((nz - 1, atoms, width), bf16),
            pltpu.VMEM((halo, width), bf16),
            dma((nz,)),
            dma((nz,)),
            dma((3 + na - 1, 3, 3)),
            dma((na, 3, 3)),
            dma(()),
        ],
        compiler_params=pltpu.CompilerParams(collective_id=1, has_side_effects=True),
        name="update_blocks",
    )(partial_sums, features, index, w_update)

    slot = slots_of(nx)
    chosen = [
        blocks[slot[a], b, c]
        for a in range(3)
        for b in range(3)
        for c in range(3)
        if (a, b, c) != (1, 1, 1)
    ]
    return new_rows, jnp.stack(chosen)


def solution(mesh):
    sizes = tuple(mesh.shape[name] for name in AXES)
    in_specs = (
        P(AXES, None),
        P(AXES),
        P(AXES, None),
        P(AXES, None),
        P(AXES),
        P(AXES, None),
        P("gz", None, None),
        P("gz", None, None),
        P(),
    )
    out_specs = (P(AXES, None), P(AXES, None, None))
    return jax.shard_map(
        functools.partial(shards, sizes), mesh=mesh, in_specs=in_specs, out_specs=out_specs, check_vma=False
    )
```

time: 245 us -> 108 us (0.44)
  waiting for transfers between devices: 99.1 us -> 0 us
  Pallas kernels: 0 us -> 89.6 us
  blocking collectives: 72.1 us -> 0 us
  starting transfers between devices: 25.8 us -> 0 us
  matrix products: 20.5 us -> 0 us
  other arithmetic: 6.8 us -> 2.19 us
  local copies, waits for them, and re-layouts: 17.2 us -> 14.7 us
    ppermute x12 -> x0, waiting for transfers between devices: 99.1 us -> none  [the longest x6 52.5 us: extended(): before = lax.ppermute(last, axis, up)]
    pallas_call x0 -> x3, Pallas kernels: none -> 89.6 us  [the longest x1 38.1 us: shards(): pl.pallas_call(functools.partial(gather_kernel, sizes), out_shape=(jax.Sh...]
    all_gather x1 -> x0, blocking collectives: 44.4 us -> none  [shards(): owners = lax.all_gather(features, 'gz', axis=0, tiled=True)]
    all_to_all x1 -> x0, blocking collectives: 27.7 us -> none  [shards(): lax.all_to_all(partial_value, 'gz', split_axis=0, concat_axis=0, tiled=True)]
    dot_general x5 -> x0, matrix products: 20.5 us -> none  [the longest x1 7.98 us: shards(): jnp.einsum('och,hd->ocd', hidden, w_second, preferred_element_type=jnp.fl...]
    gather x4 -> x0, local copies, waits for them, and re-layouts: 15.5 us -> none  [the longest x1 7.59 us: shards(): src_rows = table_rows[edge_src]]
    ppermute x12 -> x0, starting transfers between devices: 14 us -> none  [the longest x6 12.8 us: extended(): after = lax.ppermute(first, axis, down)]
    unnamed x19 -> x32, local copies, waits for them, and re-layouts: 0.71 us -> 13.4 us
  transfers between devices with their start and end apart: 15 -> 0, of which waited for: 12 -> 0; matrix products, arithmetic and copies ran while one was open for 12% -> 0% of each run, Pallas kernels for 0% -> 0%
where the time goes in v1:
time: 108 us; the launch traced here: 107 us
  Pallas kernels  89.6 us (83%)
  local copies, waits for them, and re-layouts  14.7 us (14%)
  other arithmetic  2.19 us (2%)
    pallas_call x1, Pallas kernels, shards(): pl.pallas_call(functools.partial(gather_kernel, sizes), out_shape=(jax.Sh...  38.1 us
    pallas_call x1, Pallas kernels, shards(): pl.pallas_call(functools.partial(update_kernel, sizes, halo), out_shape=(...  33.2 us
    pallas_call x1, Pallas kernels, shards(): pl.pallas_call(functools.partial(edge_kernel, nz, halo), out_shape=jax.Sh...  18.3 us
    unnamed x32, local copies, waits for them, and re-layouts  13.4 us

profile of v1, /device:TPU:1, one launch (start us, length us, event | category | flops | bytes accessed | tf_op | source)
XLA Modules:
  0.0 107.2 jit_solution(5696899032466514724)
XLA Ops:
  0.6 0.7 convert_bitcast_fusion
  1.3 0.6 pad.8.h_ref
  1.9 0.7 fusion.12
  2.6 0.8 fusion.11
  3.4 0.6 pad.9.meta_ref
  4.1 38.1 %gather_blocks.1 = (bf16[2,3,4,128,512]{4,3,2,1,0:T(8,128)(2,1)}, f32[2,3,4,8,128]{4,3,2,1,0:T(8,128)}, bf16[4,384,128]{2,1,0:T(8,128)(2,1)}, f32[4,8,384]{2,1,0:T(8,128)}) custom-call(bf16[128,512]{1,0:T(8,128)(2,1)} %f_ref.3, f32[8,128]{1,0:T(8,128)} %pad.8.h_ref, bf16[4,384,128]{2,1,0:T(8,128)(2,1)} %bitcast.52, f32[4,8,384]{2,1,0:T(8,128)} %pad.9.meta_ref), custom_call_target="tpu_custom_call" | custom-call | tf_op jit(solution)/shard_map/gather_blocks/pallas_call | solution.py:352
  42.1 18.3 %edge_network.1.part_ref = bf16[4,128,512]{2,1,0:T(8,128)(2,1)} custom-call(bf16[2,3,4,128,512]{4,3,2,1,0:T(8,128)(2,1)} %get-tuple-element.8.g_ref, f32[2,3,4,8,128]{4,3,2,1,0:T(8,128)} %get-tuple-element.9.hg_ref, bf16[4,384,128]{2,1,0:T(8,128)(2,1)} %get-tuple-element.10.bg_ref, f32[4,8,384]{2,1,0:T(8,128)} %get-tuple-element.11.mg_ref, ...), custom_call_target="tpu_custom_call" | custom-call | tf_op jit(solution)/shard_map/edge_network/pallas_call | solution.py:376
  60.5 33.2 %update_blocks.1 = (bf16[128,512]{1,0:T(8,128)(2,1)}, bf16[2,3,3,96,512]{4,3,2,1,0:T(8,128)(2,1)}) custom-call(bf16[4,128,512]{2,1,0:T(8,128)(2,1)} %edge_network.1.part_ref, bf16[128,512]{1,0:T(8,128)(2,1)} %f_ref.3, f32[8,128]{1,0:T(8,128)} %pad.8.h_ref, bf16[512,512]{1,0:T(8,128)(2,1)} %w_ref.1), custom_call_target="tpu_custom_call" | custom-call | tf_op jit(solution)/shard_map/update_blocks/pallas_call | solution.py:389
  93.7 1.0 bitcast_dynamic-update-slice_fusion.24
  94.7 0.9 bitcast_dynamic-update-slice_fusion.22
  95.6 0.9 bitcast_dynamic-update-slice_fusion.20
  96.5 0.9 bitcast_dynamic-update-slice_fusion.18
  97.4 0.9 bitcast_dynamic-update-slice_fusion.16
  98.3 0.9 bitcast_dynamic-update-slice_fusion.14
  99.2 0.9 bitcast_dynamic-update-slice_fusion.12
  100.1 0.9 bitcast_dynamic-update-slice_fusion.10
  101.0 0.9 bitcast_dynamic-update-slice_fusion.8
  101.9 0.9 bitcast_dynamic-update-slice_fusion.7
  102.8 0.9 bitcast_dynamic-update-slice_fusion.6
  103.7 0.9 bitcast_dynamic-update-slice_fusion.5
  104.6 0.9 bitcast_dynamic-update-slice_fusion.4
  105.7 0.0 copy-start.2
  105.7 0.7 copy.38
  106.4 0.8 copy-done.2
  (20 shorter events, 0.2 us)
Async XLA Ops:
  93.6 11.9 %copy-start = (bf16[2,3,3,96,512]{4,3,2,1,0:T(8,128)(2,1)S(1)}, bf16[2,3,3,96,512]{4,3,2,1,0:T(8,128)(2,1)}, u32[]{:S(2)}) copy-start(bf16[2,3,3,96,512]{4,3,2,1,0:T(8,128)(2,1)} %get-tuple-element.13) | copy-start | bytes 5308420
  93.7 12.1 %copy-start.1 = (bf16[128,512]{1,0:T(8,128)(2,1)S(1)}, bf16[128,512]{1,0:T(8,128)(2,1)}, u32[]{:S(2)}) copy-start(bf16[128,512]{1,0:T(8,128)(2,1)} %get-tuple-element.16) | copy-start | bytes 393220
  105.7 1.5 %copy-start.2 = (bf16[26,96,512]{2,1,0:T(8,128)(2,1)}, bf16[26,96,512]{2,1,0:T(8,128)(2,1)S(1)}, u32[]{:S(2)}) copy-start(bf16[26,96,512]{2,1,0:T(8,128)(2,1)S(1)} %bitcast_dynamic-update-slice_fusion.9) | copy-start | bytes 7667716

commit v2 on v1

v2 whole, which is shorter than its diff:
```python
import functools

import jax
import jax.numpy as jnp
from jax import lax
from jax.experimental import pallas as pl
from jax.experimental.pallas import tpu as pltpu
from jax.sharding import PartitionSpec as P

AXES = ("gx", "gy", "gz")
MESH = pl.DeviceIdType.MESH


class Place:
    def __init__(self, sizes):
        self.nx, self.ny, self.nz = sizes
        self.x, self.y, self.z = (lax.axis_index(name) for name in AXES)
        x, y, z = self.x, self.y, self.z
        self.first = (x, y + 1 - 2 * lax.rem(y, 2), z)
        self.second = (x, lax.rem(y + 2, 4), z)
        self.b_first = 2 - 2 * lax.rem(y, 2)
        self.b_second = 2 * lax.rem(y, 2)
        self.siblings = [(lax.rem(x + 1, self.nx), y, z)]
        if self.nx > 2:
            self.siblings.append((lax.rem(x + self.nx - 1, self.nx), y, z))

    def along_z(self, step):
        return (self.x, self.y, lax.rem(self.z + step + self.nz, self.nz))

    def sibling_slot(self, index):
        return 1 if self.nx == 2 else 2 - index

    def meet(self):
        barrier = pltpu.get_barrier_semaphore()
        partners = [self.along_z(step) for step in range(1, self.nz)]
        partners += [self.first, self.second] + self.siblings
        for partner in partners:
            pl.semaphore_signal(barrier, inc=1, device_id=partner, device_id_type=MESH)
        pl.semaphore_wait(barrier, len(partners))


def remote(source, target, send, receive, device):
    return pltpu.make_async_remote_copy(
        src_ref=source,
        dst_ref=target,
        send_sem=send,
        recv_sem=receive,
        device_id=device,
        device_id_type=MESH,
    )


def layer_kernel(sizes, f_ref, index_ref, src_ref, dst_ref, count_ref, basis_ref, w1_hbm, w2_hbm, w3_hbm,
                 new_ref, out_ref,
                 h_ref, meta_ref, g_ref, hg_ref, bg_ref, mg_ref, w1_ref, w2_ref, w3_ref, table, w_mix,
                 part_ref, landed, edge_rows, n_ref,
                 send, receive, e_send, e_receive, local, p_send, p_receive, n_send, n_receive, o_sem):
    place = Place(sizes)
    z, nz = place.z, place.nz
    halo = index_ref.shape[1]
    na = g_ref.shape[0]
    atoms, width = g_ref.shape[3:]
    groups, slots = src_ref.shape
    radial = bg_ref.shape[2]
    lanes = hg_ref.shape[4]
    group = na * 3 * halo
    f32, bf16 = jnp.float32, jnp.bfloat16
    pairs = ((f_ref, g_ref), (h_ref, hg_ref))
    edge_pairs = ((meta_ref, mg_ref), (basis_ref, bg_ref))

    weights = [
        pltpu.make_async_copy(w1_hbm, w1_ref, local.at[0]),
        pltpu.make_async_copy(w2_hbm, w2_ref, local.at[1]),
        pltpu.make_async_copy(w3_hbm, w3_ref, local.at[2]),
    ]
    own_basis = pltpu.make_async_copy(basis_ref.at[z], bg_ref.at[z], local.at[3])
    for copy in weights + [own_basis]:
        copy.start()

    h_ref[...] = jnp.full(h_ref.shape, -1.0, f32)
    h_ref[0:1, :halo] = index_ref[...].astype(f32)
    edge_src = src_ref[...].astype(f32)
    beyond = edge_src - float(atoms)
    offset = jnp.floor((beyond + 0.5) * (1.0 / halo))
    slot = beyond - offset * float(halo)
    offset = jnp.where(offset >= 13.0, offset + 1.0, offset)
    off_x = jnp.floor((offset + 0.5) * (1.0 / 9.0))
    inner = offset - 9.0 * off_x
    off_y = jnp.floor((inner + 0.5) * (1.0 / 3.0))
    off_z = inner - 3.0 * off_y
    slot_x = jnp.where(off_x == 1.0, 0.0, jnp.where(off_x == 2.0, 1.0, float(na - 1)))
    position = float(atoms) + ((off_z * float(na) + slot_x) * 3.0 + off_y) * float(halo) + slot
    position = jnp.where(edge_src < float(atoms), edge_src, position)
    row_lane = lax.broadcasted_iota(jnp.int32, (1, slots), 1)
    meta_ref[...] = jnp.zeros_like(meta_ref)
    for j in range(groups):
        meta_ref[j, 0:1, :] = position[j : j + 1, :]
        target = jnp.where(row_lane < count_ref[j], dst_ref[j : j + 1, :], -1)
        meta_ref[j, 1:2, :] = target.astype(f32)
    g_ref[0, 1, z] = f_ref[...]
    hg_ref[0, 1, z] = h_ref[...]
    mg_ref[z] = meta_ref[z]
    place.meet()

    def when(entry, action):
        s, sign = entry
        zz = z + sign * s
        if s == 0:
            action(zz)
        else:
            pl.when((zz >= 0) & (zz < nz))(functools.partial(action, zz))

    def transfers(s, b, zz, kind, slot, device):
        out = []
        for q, (own, grid) in enumerate(pairs):
            index = 1 if b is None else b
            source = own if (s == 0 and b is None) else grid.at[0, index, zz]
            out.append(remote(source, grid.at[slot[0], slot[1], zz], send.at[q, kind, index, zz],
                              receive.at[q, slot[0], slot[1], zz], device))
        return out

    def to_siblings(s, b, zz):
        out = []
        for i, device in enumerate(place.siblings):
            slot = (place.sibling_slot(i), 1 if b is None else b)
            out += transfers(s, b, zz, 4 + i, slot, device)
        return out

    def arrival(a, b, zz):
        for q, (own, grid) in enumerate(pairs):
            remote(grid.at[a, b, zz], grid.at[a, b, zz], send.at[q, 0, 0, 0],
                   receive.at[q, a, b, zz], place.first).wait_recv()

    def chain(entry, zz, do):
        s, sign = entry
        if s < nz - 1:
            for go in ((1, -1) if s == 0 else (-sign,)):
                device = (place.x, place.y, z + go)

                def act():
                    for copy in transfers(s, None, zz, 0 if go > 0 else 1, (0, 1), device):
                        do(copy)

                pl.when((z + go >= 0) & (z + go < nz))(act)

    def own_stage(entry, do):
        def act(zz):
            if entry[0] > 0 and do is start:
                arrival(0, 1, zz)
            chain(entry, zz, do)
            for copy in transfers(entry[0], None, zz, 2, (0, place.b_second), place.first):
                do(copy)
            for copy in to_siblings(entry[0], None, zz):
                do(copy)

        when(entry, act)

    def first_stage(entry, do):
        def act(zz):
            if do is start:
                arrival(0, place.b_first, zz)
            for copy in transfers(1, place.b_first, zz, 3, (0, place.b_second), place.second):
                do(copy)
            for copy in to_siblings(1, place.b_first, zz):
                do(copy)

        when(entry, act)

    def second_stage(entry, do):
        def act(zz):
            if do is start:
                arrival(0, place.b_second, zz)
            for copy in to_siblings(1, place.b_second, zz):
                do(copy)

        when(entry, act)

    def edges(q, do):
        own, grid = edge_pairs[q]
        for step in range(1, nz):
            device = place.along_z(step)
            do(remote(own.at[device[2]], grid.at[z], e_send.at[q, step], e_receive.at[q, step], device))

    def start(copy):
        copy.start()

    def finish(copy):
        copy.wait_send()

    rounds = [[(0, 0)]] + [[(s, -1), (s, 1)] for s in range(1, nz)]
    for r in range(nz + 2):
        if r < nz:
            for entry in rounds[r]:
                own_stage(entry, start)
        if r == 0:
            edges(0, start)
        if r == nz - 1:
            edges(1, start)
        if 1 <= r <= nz:
            for entry in rounds[r - 1]:
                first_stage(entry, start)
        if r >= 2:
            for entry in rounds[r - 2]:
                second_stage(entry, start)
    for copy in weights + [own_basis]:
        copy.wait()
    w_mix[:radial, :] = w1_ref[2 * width :, :]
    rest = table.shape[0] - (nz + 2) * group
    table[(nz + 2) * group :, :] = jnp.zeros((rest, width), bf16)
    for a in range(1, na):
        for b in range(3):
            for zz in range(nz):
                arrival(a, b, zz)
    edges(0, lambda copy: copy.wait_recv())
    edges(1, lambda copy: copy.wait_recv())

    lane = lax.broadcasted_iota(jnp.int32, (lanes, lanes), 1).astype(f32)

    def boundary(index_row, rows):
        index = jnp.broadcast_to(index_row, (lanes, lanes)).T
        pick = (index == lane).astype(bf16)[:halo, :atoms]
        return jnp.dot(pick, rows, preferred_element_type=f32).astype(bf16)

    def fill(zz, carry):
        for a in range(na):
            for b in range(3):
                rows = boundary(hg_ref[a, b, zz, 0:1, :], g_ref[a, b, zz])
                at = (a * 3 + b) * halo
                table[pl.ds(pl.multiple_of((zz + 1) * group + at, 16), halo), :] = rows

                @pl.when(zz == 0)
                def _():
                    table[pl.ds((nz + 1) * group + at, halo), :] = rows

                @pl.when(zz == nz - 1)
                def _():
                    table[pl.ds(at, halo), :] = rows
        return carry

    lax.fori_loop(0, nz, fill, 0)
    window = -(-3 * group // lanes) * lanes
    lane_s = lax.broadcasted_iota(jnp.int32, (slots, lanes), 1).astype(f32)
    sublane = lax.broadcasted_iota(jnp.int32, (atoms, slots), 0).astype(f32)

    def domain(o):
        position = jnp.broadcast_to(mg_ref[o, 0:1, :], (lanes, slots)).T
        target = jnp.broadcast_to(mg_ref[o, 1:2, :], (lanes, slots)).T
        own = g_ref[0, 1, o]
        pick = (position == lane_s).astype(bf16)
        source = jnp.dot(pick, own, preferred_element_type=f32)
        picks = jnp.concatenate(
            [(position - float(atoms + j * lanes) == lane_s).astype(bf16) for j in range(window // lanes)],
            axis=1,
        )
        rows = table[pl.ds(pl.multiple_of(o * group, 16), window), :]
        source = source + jnp.dot(picks, rows, preferred_element_type=f32)
        w_mix[radial:, :] = jnp.dot(
            own, w1_ref[width : 2 * width, :], preferred_element_type=f32
        ).astype(bf16)
        mix = jnp.concatenate([bg_ref[o], (target == lane_s).astype(bf16)], axis=1)
        pre = jnp.dot(source.astype(bf16), w1_ref[:width, :], preferred_element_type=f32)
        pre = pre + jnp.dot(mix, w_mix[...], preferred_element_type=f32)
        half = 0.5 * pre
        hidden = (half + half * jnp.tanh(half)).astype(bf16)
        incidence = (jnp.broadcast_to(mg_ref[o, 1:2, :], (atoms, slots)) == sublane).astype(bf16)
        summed = jnp.dot(incidence, hidden, preferred_element_type=f32).astype(bf16)
        return jnp.dot(summed, w2_ref[...], preferred_element_type=f32)

    def returned(step):
        device = place.along_z(step + 1)
        return remote(part_ref.at[step], landed.at[step], p_send.at[step], p_receive.at[step], device)

    def other(step, carry):
        part_ref[step] = domain(lax.rem(z + step + 1, nz)).astype(bf16)
        returned(step).start()
        return carry

    lax.fori_loop(0, nz - 1, other, 0)
    total = domain(z)
    for step in range(nz - 1):
        returned(step).wait_recv()
        total = total + landed[step].astype(f32)
    mean_square = jnp.mean(total * total, axis=-1, keepdims=True)
    normed = (total * lax.rsqrt(mean_square + 1e-05)).astype(bf16)
    update = jnp.dot(normed, w3_ref[...], preferred_element_type=f32)
    new_rows = (f_ref[...].astype(f32) + update).astype(bf16)
    edge_rows[...] = boundary(h_ref[0:1, :], new_rows)
    new_ref[...] = new_rows

    started = []
    written = []

    def begin(b, c, kind, slot, device):
        source = edge_rows if (b is None and c == 1) else n_ref.at[0, 1 if b is None else b, c]
        index = 1 if b is None else b
        copy = remote(source, n_ref.at[slot], n_send.at[kind, index, c], n_receive.at[slot], device)
        copy.start()
        started.append(copy)

    def landing(a, b, c):
        remote(n_ref.at[a, b, c], n_ref.at[a, b, c], n_send.at[0, 0, 0], n_receive.at[a, b, c], place.first).wait_recv()

    def write(a, b, c):
        for part, slot in enumerate((1, 0, 1) if na == 2 else (2, 0, 1)):
            if slot == a:
                cell = part * 9 + b * 3 + c
                cell = cell - 1 if isinstance(cell, int) and cell > 13 else cell
                if not isinstance(cell, int):
                    cell = jnp.where(cell > 13, cell - 1, cell)
                copy = pltpu.make_async_copy(n_ref.at[a, b, c], out_ref.at[cell], o_sem.at[cell])
                copy.start()
                written.append(copy)

    def to_siblings_next(b, c):
        for i, device in enumerate(place.siblings):
            begin(b, c, 3 + i, (place.sibling_slot(i), 1 if b is None else b, c), device)

    begin(None, 1, 0, (0, 1, 0), place.along_z(1))
    begin(None, 1, 1, (0, 1, 2), place.along_z(-1))
    begin(None, 1, 2, (0, place.b_second, 1), place.first)
    to_siblings_next(None, 1)
    order = (1, 0, 2)
    for c in order[1:]:
        landing(0, 1, c)
        begin(None, c, 2, (0, place.b_second, c), place.first)
        to_siblings_next(None, c)
        write(0, 1, c)
    for c in order:
        landing(0, place.b_first, c)
        begin(place.b_first, c, 2, (0, place.b_second, c), place.second)
        to_siblings_next(place.b_first, c)
        write(0, place.b_first, c)
    for c in order:
        landing(0, place.b_second, c)
        to_siblings_next(place.b_second, c)
        write(0, place.b_second, c)
    for b in (1, place.b_first, place.b_second):
        for a in range(1, na):
            for c in order:
                landing(a, b, c)
                write(a, b, c)
    for group_ in rounds:
        for entry in group_:
            own_stage(entry, finish)
            first_stage(entry, finish)
            second_stage(entry, finish)
    for q in range(2):
        edges(q, finish)
    for step in range(nz - 1):
        returned(step).wait_send()
    for copy in started:
        copy.wait_send()
    for copy in written:
        copy.wait()


def shards(sizes, features, halo_index, edge_src, edge_dst, edge_count, edge_basis, w_edge_in, w_edge_out, w_update):
    nx, ny, nz = sizes
    atoms, width = features.shape
    groups, slots = edge_src.shape
    halo = halo_index.shape[0]
    radial = edge_basis.shape[1]
    hidden = w_edge_in.shape[2]
    lanes = -(-max(atoms, halo) // 128) * 128
    na = 2 if nx == 2 else 3
    f32, bf16 = jnp.float32, jnp.bfloat16
    basis = edge_basis.reshape(groups, slots, radial)
    vmem = pl.BlockSpec(memory_space=pltpu.VMEM)
    smem = pl.BlockSpec(memory_space=pltpu.SMEM)
    anywhere = pl.BlockSpec(memory_space=pl.ANY)
    dma = pltpu.SemaphoreType.DMA
    kinds = 4 + (na - 1)
    group = na * 3 * halo
    window = -(-3 * group // lanes) * lanes
    table_rows = (nz - 1) * group + window
    new_rows, blocks = pl.pallas_call(
        functools.partial(layer_kernel, sizes),
        out_shape=(
            jax.ShapeDtypeStruct((atoms, width), bf16),
            jax.ShapeDtypeStruct((26, halo, width), bf16),
        ),
        in_specs=[vmem, vmem, vmem, vmem, smem, anywhere, anywhere, anywhere, anywhere],
        out_specs=(vmem, anywhere),
        scratch_shapes=[
            pltpu.VMEM((8, lanes), f32),
            pltpu.VMEM((nz, 8, slots), f32),
            pltpu.VMEM((na, 3, nz, atoms, width), bf16),
            pltpu.VMEM((na, 3, nz, 8, lanes), f32),
            pltpu.VMEM((nz, slots, radial), bf16),
            pltpu.VMEM((nz, 8, slots), f32),
            pltpu.VMEM(w_edge_in.shape[1:], bf16),
            pltpu.VMEM(w_edge_out.shape[1:], bf16),
            pltpu.VMEM(w_update.shape, bf16),
            pltpu.VMEM((table_rows, width), bf16),
            pltpu.VMEM((radial + lanes, hidden), bf16),
            pltpu.VMEM((nz - 1, atoms, width), bf16),
            pltpu.VMEM((nz - 1, atoms, width), bf16),
            pltpu.VMEM((halo, width), bf16),
            pltpu.VMEM((na, 3, 3, halo, width), bf16),
            dma((2, kinds, 3, nz)),
            dma((2, na, 3, nz)),
            dma((2, nz)),
            dma((2, nz)),
            dma((4,)),
            dma((nz - 1,)),
            dma((nz - 1,)),
            dma((3 + na - 1, 3, 3)),
            dma((na, 3, 3)),
            dma((26,)),
        ],
        compiler_params=pltpu.CompilerParams(
            collective_id=0, has_side_effects=True, vmem_limit_bytes=60 * 1024 * 1024
        ),
        name="layer",
    )(features, halo_index.reshape(1, halo), edge_src, edge_dst, edge_count, basis,
      w_edge_in[0], w_edge_out[0], w_update)
    return new_rows, blocks


def solution(mesh):
    sizes = tuple(mesh.shape[name] for name in AXES)
    in_specs = (
        P(AXES, None),
        P(AXES),
        P(AXES, None),
        P(AXES, None),
        P(AXES),
        P(AXES, None),
        P("gz", None, None),
        P("gz", None, None),
        P(),
    )
    out_specs = (P(AXES, None), P(AXES, None, None))
    return jax.shard_map(
        functools.partial(shards, sizes), mesh=mesh, in_specs=in_specs, out_specs=out_specs, check_vma=False
    )
```

time: 108 us -> 74.3 us (0.69)
  Pallas kernels: 89.6 us -> 68.5 us
  local copies, waits for them, and re-layouts: 14.7 us -> 5.01 us
  other arithmetic: 2.19 us -> 0 us
    pallas_call x3 -> x1, Pallas kernels: 89.6 us -> 68.5 us  [shards(): pl.pallas_call(functools.partial(layer_kernel, sizes), out_shape=(jax.Sha...]
    unnamed x32 -> x2, local copies, waits for them, and re-layouts: 13.4 us -> 5.01 us
    pad x2 -> x0, local copies, waits for them, and re-layouts: 1.22 us -> none  [the longest x1 0.63 us: shards(): meta = jnp.pad(meta, ((0, 0), (0, 6), (0, 0)))]
where the time goes in v2:
time: 74.3 us; the launch traced here: 74.1 us
  Pallas kernels  68.5 us (92%)
  local copies, waits for them, and re-layouts  5.01 us (7%)
    pallas_call x1, Pallas kernels, shards(): pl.pallas_call(functools.partial(layer_kernel, sizes), out_shape=(jax.Sha...  68.5 us
    unnamed x2, local copies, waits for them, and re-layouts  5.01 us

profile of v2, /device:TPU:1, one launch (start us, length us, event | category | flops | bytes accessed | tf_op | source)
XLA Modules:
  0.0 74.1 jit_solution(2520783132617517814)
XLA Ops:
  0.6 68.5 %layer.1 = (bf16[128,512]{1,0:T(8,128)(2,1)}, bf16[26,96,512]{2,1,0:T(8,128)(2,1)}) custom-call(bf16[128,512]{1,0:T(8,128)(2,1)} %f_ref.1, s32[1,96]{1,0:T(1,128)} %bitcast.7, s32[4,384]{1,0:T(4,128)} %src_ref.1, s32[4,384]{1,0:T(4,128)} %dst_ref.1, s32[4]{0:T(128)} %count_ref.1, bf16[4,384,128]{2,1,0:T(8,128)(2,1)} %bitcast.6, bf16[1152,1024]{1,0:T(8,128)(2,1)} %bitcast.4, ...), custom_call_target="tpu_custom_call" | custom-call | tf_op jit(solution)/shard_map/layer/pallas_call | solution.py:376
  69.1 1.6 %copy.13 = bf16[128,512]{1,0:T(8,128)(2,1)} copy(bf16[128,512]{1,0:T(8,128)(2,1)} %get-tuple-element.4) | data formatting | bytes 262144
  70.7 3.4 %copy.14 = bf16[26,96,512]{2,1,0:T(8,128)(2,1)} copy(bf16[26,96,512]{2,1,0:T(8,128)(2,1)} %get-tuple-element.5) | data formatting | bytes 5111808

commit v3 on v2

--- a/solution.py
+++ b/solution.py
@@ -53,7 +53,7 @@
 def layer_kernel(sizes, f_ref, index_ref, src_ref, dst_ref, count_ref, basis_ref, w1_hbm, w2_hbm, w3_hbm,
                  new_ref, out_ref,
                  h_ref, meta_ref, g_ref, hg_ref, bg_ref, mg_ref, w1_ref, w2_ref, w3_ref, table, w_mix,
-                 part_ref, landed, edge_rows, n_ref,
+                 part_ref, landed, edge_rows, fresh, n_ref,
                  send, receive, e_send, e_receive, local, p_send, p_receive, n_send, n_receive, o_sem):
     place = Place(sizes)
     z, nz = place.z, place.nz
@@ -187,11 +187,33 @@
     def finish(copy):
         copy.wait_send()
 
+    lane = lax.broadcasted_iota(jnp.int32, (lanes, lanes), 1).astype(f32)
+
+    def boundary(index_row, rows):
+        index = jnp.broadcast_to(index_row, (lanes, lanes)).T
+        pick = (index == lane).astype(bf16)[:halo, :atoms]
+        return jnp.dot(pick, rows, preferred_element_type=f32).astype(bf16)
+
+    def fill(a, b, zz):
+        rows = boundary(hg_ref[a, b, zz, 0:1, :], g_ref[a, b, zz])
+        at = pl.multiple_of((a * 3 + b) * halo, 16)
+        table[pl.ds(pl.multiple_of((zz + 1) * group + at, 16), halo), :] = rows
+
+        @pl.when(zz == 0)
+        def _():
+            table[pl.ds(pl.multiple_of((nz + 1) * group + at, 16), halo), :] = rows
+
+        @pl.when(zz == nz - 1)
+        def _():
+            table[pl.ds(at, halo), :] = rows
+
     rounds = [[(0, 0)]] + [[(s, -1), (s, 1)] for s in range(1, nz)]
     for r in range(nz + 2):
+        landed_now = []
         if r < nz:
             for entry in rounds[r]:
                 own_stage(entry, start)
+                landed_now.append((entry, 1))
         if r == 0:
             edges(0, start)
         if r == nz - 1:
@@ -199,45 +221,38 @@
         if 1 <= r <= nz:
             for entry in rounds[r - 1]:
                 first_stage(entry, start)
+                landed_now.append((entry, place.b_first))
         if r >= 2:
             for entry in rounds[r - 2]:
                 second_stage(entry, start)
+                landed_now.append((entry, place.b_second))
+        for entry, b in landed_now:
+            when(entry, functools.partial(fill, 0, b))
     for copy in weights + [own_basis]:
         copy.wait()
-    w_mix[:radial, :] = w1_ref[2 * width :, :]
     rest = table.shape[0] - (nz + 2) * group
     table[(nz + 2) * group :, :] = jnp.zeros((rest, width), bf16)
+
+    def project(o, carry):
+        w_mix[o, :radial, :] = w1_ref[2 * width :, :]
+        w_mix[o, radial:, :] = jnp.dot(
+            g_ref[0, 1, o], w1_ref[width : 2 * width, :], preferred_element_type=f32
+        ).astype(bf16)
+        return carry
+
+    lax.fori_loop(0, nz, project, 0)
     for a in range(1, na):
-        for b in range(3):
-            for zz in range(nz):
-                arrival(a, b, zz)
+        for step in range(nz):
+
+            def last(zz, a=a):
+                for b in (1, place.b_first, place.b_second):
+                    arrival(a, b, zz)
+                    fill(a, b, zz)
+
+            for entry in rounds[step]:
+                when(entry, last)
     edges(0, lambda copy: copy.wait_recv())
     edges(1, lambda copy: copy.wait_recv())
-
-    lane = lax.broadcasted_iota(jnp.int32, (lanes, lanes), 1).astype(f32)
-
-    def boundary(index_row, rows):
-        index = jnp.broadcast_to(index_row, (lanes, lanes)).T
-        pick = (index == lane).astype(bf16)[:halo, :atoms]
-        return jnp.dot(pick, rows, preferred_element_type=f32).astype(bf16)
-
-    def fill(zz, carry):
-        for a in range(na):
-            for b in range(3):
-                rows = boundary(hg_ref[a, b, zz, 0:1, :], g_ref[a, b, zz])
-                at = (a * 3 + b) * halo
-                table[pl.ds(pl.multiple_of((zz + 1) * group + at, 16), halo), :] = rows
-
-                @pl.when(zz == 0)
-                def _():
-                    table[pl.ds((nz + 1) * group + at, halo), :] = rows
-
-                @pl.when(zz == nz - 1)
-                def _():
-                    table[pl.ds(at, halo), :] = rows
-        return carry
-
-    lax.fori_loop(0, nz, fill, 0)
     window = -(-3 * group // lanes) * lanes
     lane_s = lax.broadcasted_iota(jnp.int32, (slots, lanes), 1).astype(f32)
     sublane = lax.broadcasted_iota(jnp.int32, (atoms, slots), 0).astype(f32)
@@ -254,12 +269,9 @@
         )
         rows = table[pl.ds(pl.multiple_of(o * group, 16), window), :]
         source = source + jnp.dot(picks, rows, preferred_element_type=f32)
-        w_mix[radial:, :] = jnp.dot(
-            own, w1_ref[width : 2 * width, :], preferred_element_type=f32
-        ).astype(bf16)
         mix = jnp.concatenate([bg_ref[o], (target == lane_s).astype(bf16)], axis=1)
         pre = jnp.dot(source.astype(bf16), w1_ref[:width, :], preferred_element_type=f32)
-        pre = pre + jnp.dot(mix, w_mix[...], preferred_element_type=f32)
+        pre = pre + jnp.dot(mix, w_mix[o], preferred_element_type=f32)
         half = 0.5 * pre
         hidden = (half + half * jnp.tanh(half)).astype(bf16)
         incidence = (jnp.broadcast_to(mg_ref[o, 1:2, :], (atoms, slots)) == sublane).astype(bf16)
@@ -285,7 +297,9 @@
     update = jnp.dot(normed, w3_ref[...], preferred_element_type=f32)
     new_rows = (f_ref[...].astype(f32) + update).astype(bf16)
     edge_rows[...] = boundary(h_ref[0:1, :], new_rows)
-    new_ref[...] = new_rows
+    fresh[...] = new_rows
+    keep = pltpu.make_async_copy(fresh, new_ref, local.at[0])
+    keep.start()
 
     started = []
     written = []
@@ -301,15 +315,9 @@
         remote(n_ref.at[a, b, c], n_ref.at[a, b, c], n_send.at[0, 0, 0], n_receive.at[a, b, c], place.first).wait_recv()
 
     def write(a, b, c):
-        for part, slot in enumerate((1, 0, 1) if na == 2 else (2, 0, 1)):
-            if slot == a:
-                cell = part * 9 + b * 3 + c
-                cell = cell - 1 if isinstance(cell, int) and cell > 13 else cell
-                if not isinstance(cell, int):
-                    cell = jnp.where(cell > 13, cell - 1, cell)
-                copy = pltpu.make_async_copy(n_ref.at[a, b, c], out_ref.at[cell], o_sem.at[cell])
-                copy.start()
-                written.append(copy)
+        copy = pltpu.make_async_copy(n_ref.at[a, b, c], out_ref.at[a, b, c], o_sem.at[a, b, c])
+        copy.start()
+        written.append(copy)
 
     def to_siblings_next(b, c):
         for i, device in enumerate(place.siblings):
@@ -319,6 +327,9 @@
     begin(None, 1, 1, (0, 1, 2), place.along_z(-1))
     begin(None, 1, 2, (0, place.b_second, 1), place.first)
     to_siblings_next(None, 1)
+    centre = pltpu.make_async_copy(edge_rows, out_ref.at[0, 1, 1], o_sem.at[0, 1, 1])
+    centre.start()
+    written.append(centre)
     order = (1, 0, 2)
     for c in order[1:]:
         landing(0, 1, c)
@@ -350,7 +361,37 @@
         returned(step).wait_send()
     for copy in started:
         copy.wait_send()
+    keep.wait()
     for copy in written:
+        copy.wait()
+
+
+def spread_kernel(new_ref, blocks_ref, new_out, out_ref, rows, blocks, row_sem, in_sem, out_sem):
+    na = blocks_ref.shape[0]
+    parts = (1, 0, 1) if na == 2 else (2, 0, 1)
+    first = pltpu.make_async_copy(new_ref, rows, row_sem.at[0])
+    last = pltpu.make_async_copy(rows, new_out, row_sem.at[1])
+    loads = [
+        (a, b, pltpu.make_async_copy(blocks_ref.at[a, b], blocks.at[a, b], in_sem.at[a, b]))
+        for a in range(na)
+        for b in range(3)
+    ]
+    for _, _, copy in loads:
+        copy.start()
+    first.start()
+    stores = []
+    for a, b, copy in loads:
+        copy.wait()
+        for part, slot in enumerate(parts):
+            for c in range(3):
+                cell = part * 9 + b * 3 + c
+                if slot == a and cell != 13:
+                    cell = cell - 1 if cell > 13 else cell
+                    stores.append(pltpu.make_async_copy(blocks.at[a, b, c], out_ref.at[cell], out_sem.at[cell]))
+                    stores[-1].start()
+    first.wait()
+    last.start()
+    for copy in stores + [last]:
         copy.wait()
 
 
@@ -377,10 +418,10 @@
         functools.partial(layer_kernel, sizes),
         out_shape=(
             jax.ShapeDtypeStruct((atoms, width), bf16),
-            jax.ShapeDtypeStruct((26, halo, width), bf16),
+            jax.ShapeDtypeStruct((na, 3, 3, halo, width), bf16),
         ),
         in_specs=[vmem, vmem, vmem, vmem, smem, anywhere, anywhere, anywhere, anywhere],
-        out_specs=(vmem, anywhere),
+        out_specs=(anywhere, anywhere),
         scratch_shapes=[
             pltpu.VMEM((8, lanes), f32),
             pltpu.VMEM((nz, 8, slots), f32),
@@ -392,10 +433,11 @@
             pltpu.VMEM(w_edge_out.shape[1:], bf16),
             pltpu.VMEM(w_update.shape, bf16),
             pltpu.VMEM((table_rows, width), bf16),
-            pltpu.VMEM((radial + lanes, hidden), bf16),
+            pltpu.VMEM((nz, radial + lanes, hidden), bf16),
             pltpu.VMEM((nz - 1, atoms, width), bf16),
             pltpu.VMEM((nz - 1, atoms, width), bf16),
             pltpu.VMEM((halo, width), bf16),
+            pltpu.VMEM((atoms, width), bf16),
             pltpu.VMEM((na, 3, 3, halo, width), bf16),
             dma((2, kinds, 3, nz)),
             dma((2, na, 3, nz)),
@@ -406,7 +448,7 @@
             dma((nz - 1,)),
             dma((3 + na - 1, 3, 3)),
             dma((na, 3, 3)),
-            dma((26,)),
+            dma((na, 3, 3)),
         ],
         compiler_params=pltpu.CompilerParams(
             collective_id=0, has_side_effects=True, vmem_limit_bytes=60 * 1024 * 1024
@@ -414,7 +456,23 @@
         name="layer",
     )(features, halo_index.reshape(1, halo), edge_src, edge_dst, edge_count, basis,
       w_edge_in[0], w_edge_out[0], w_update)
-    return new_rows, blocks
+    return pl.pallas_call(
+        spread_kernel,
+        out_shape=(
+            jax.ShapeDtypeStruct((atoms, width), bf16),
+            jax.ShapeDtypeStruct((26, halo, width), bf16),
+        ),
+        in_specs=[anywhere, anywhere],
+        out_specs=(anywhere, anywhere),
+        scratch_shapes=[
+            pltpu.VMEM((atoms, width), bf16),
+            pltpu.VMEM((na, 3, 3, halo, width), bf16),
+            dma((2,)),
+            dma((na, 3)),
+            dma((26,)),
+        ],
+        name="spread",
+    )(new_rows, blocks)
 
 
 def solution(mesh):

time: 74.3 us -> 66.9 us (0.900); the launches traced: 74.1 us -> 65.7 us
  local copies, waits for them, and re-layouts: 5.01 us -> 0 us
  Pallas kernels: 68.5 us -> 65 us
    pallas_call x1, Pallas kernels: 68.5 us -> 62.2 us  [shards(): pl.pallas_call(functools.partial(layer_kernel, sizes), out_shape=(jax.Sha...]
    unnamed x2 -> x0, local copies, waits for them, and re-layouts: 5.01 us -> none
    pallas_call x0 -> x1, Pallas kernels: none -> 2.77 us  [shards(): pl.pallas_call(spread_kernel, out_shape=(jax.ShapeDtypeStruct((atoms, wid...]
where the time goes in v3:
time: 66.9 us; the launch traced here: 65.7 us
  Pallas kernels  65 us (97%)
    pallas_call x1, Pallas kernels, shards(): pl.pallas_call(functools.partial(layer_kernel, sizes), out_shape=(jax.Sha...  62.2 us
    pallas_call x1, Pallas kernels, shards(): pl.pallas_call(spread_kernel, out_shape=(jax.ShapeDtypeStruct((atoms, wid...  2.77 us

profile of v3, /device:TPU:1, one launch (start us, length us, event | category | flops | bytes accessed | tf_op | source)
XLA Modules:
  0.0 65.7 jit_solution(9951807725974314524)
XLA Ops:
  0.6 62.2 %layer.1 = (bf16[128,512]{1,0:T(8,128)(2,1)}, bf16[2,3,3,96,512]{4,3,2,1,0:T(8,128)(2,1)}) custom-call(bf16[128,512]{1,0:T(8,128)(2,1)} %f_ref.1, s32[1,96]{1,0:T(1,128)} %bitcast.7, s32[4,384]{1,0:T(4,128)} %src_ref.1, s32[4,384]{1,0:T(4,128)} %dst_ref.1, s32[4]{0:T(128)} %count_ref.1, bf16[4,384,128]{2,1,0:T(8,128)(2,1)} %bitcast.6, ...), custom_call_target="tpu_custom_call" | custom-call | tf_op jit(solution)/shard_map/layer/pallas_call | solution.py:417
  62.9 2.8 %spread.1 = (bf16[128,512]{1,0:T(8,128)(2,1)}, bf16[26,96,512]{2,1,0:T(8,128)(2,1)}) custom-call(bf16[128,512]{1,0:T(8,128)(2,1)} %get-tuple-element.4.new_ref, bf16[2,3,3,96,512]{4,3,2,1,0:T(8,128)(2,1)} %get-tuple-element.5.blocks_ref), custom_call_target="tpu_custom_call" | custom-call | tf_op jit(solution)/shard_map/spread/pallas_call | solution.py:459
